TPU v7x, 128 devices: a whole 4x4x4 slice. The times are simulated.
128 devices in a mesh: row: 64 (over z, y, x), pan: 2 (over core).
Axes of the slice: x: 4, y: 4, z: 4, core: 2. Of those that a mesh axis runs over, the one named last changes fastest.
Arguments:
- right_side: float32 [256, 65536], P(None, 'row'), may hold values from -6 to 6
- initial_guess: float32 [256, 65536], P(None, ('row', 'pan')), may hold values from -6 to 6
- v_factor: float32 [128, 128, 16, 512], P('row', None, 'pan'), may hold values from -0.25 to 0.25
- u_factor: float32 [128, 128, 16, 512], P('row', None, 'pan'), may hold values from -0.125 to 0.125
- tile_ranks: int32 [128, 128], P(None, 'row'), may hold values from 0 to 16
- diag_block: float32 [65536, 512], P(('row', 'pan'))
- diag_inverse: float32 [65536, 512], P(('row', 'pan'))
Outputs:
- solution: float32 [256, 65536], P(None, ('row', 'pan'))
- residual: float32 [256, 65536], P(None, ('row', 'pan'))
Inputs may be any that keep to these rules, and one draw needn't show every extreme that they name: `tile_ranks`: columns of a tile's factors from its rank on are ignored, as is the low-rank part of tile (i, i).
All inputs are finite; a program needn't handle non-finite values.
Results may differ from a plain program's by a relative error of at most 0.00017.
Values sent between devices are 32-bit elements; how exact they have to be, the bound alone decides.
A program may use at most 64 MiB of HBM per device.

v0:
```python
import jax
import jax.numpy as jnp
from jax import lax
from jax.sharding import PartitionSpec as P

ITERS = 2


def on_device(right_side, initial_guess, v_factor, u_factor, tile_ranks, diag_block, diag_inverse):
    highest = lax.Precision.HIGHEST
    pan_index = lax.axis_index("pan")
    row_index = lax.axis_index("row")
    tile_rows = v_factor.shape[0]
    tile_count = v_factor.shape[1]
    part_rank = v_factor.shape[2]
    tile_width = v_factor.shape[3]
    rhs_count = right_side.shape[0]
    own_rows = diag_block.shape[0]
    row_start = pan_index * own_rows
    tile_slot = row_start // tile_width
    components = pan_index * part_rank + jnp.arange(part_rank, dtype=jnp.int32)
    own_columns = row_index * tile_rows + jnp.arange(tile_rows, dtype=jnp.int32)
    tile_index = jnp.arange(tile_count, dtype=jnp.int32)
    off_diagonal = tile_index[:, None] != own_columns[None, :]
    rank_mask = (
        (components[None, None, :] < tile_ranks[:, :, None]) & off_diagonal[:, :, None]
    ).astype(jnp.float32)
    iterate_rows = initial_guess
    residual = initial_guess
    for iteration in range(ITERS):
        guess_full = lax.all_gather(iterate_rows, "pan", axis=1, tiled=True)
        guess_tiles = guess_full.reshape(rhs_count, tile_rows, tile_width)
        projected = jnp.einsum("cikb,rcb->ickr", v_factor, guess_tiles, precision=highest)
        projected = projected * rank_mask[:, :, :, None]
        received = lax.all_to_all(projected, "row", split_axis=0, concat_axis=1, tiled=True)
        low_rank = jnp.einsum("ickm,ickr->rim", u_factor, received, precision=highest)
        low_rank = low_rank.reshape(rhs_count, tile_rows * tile_width)
        guess_tile = lax.dynamic_slice_in_dim(guess_full, tile_slot * tile_width, tile_width, 1)
        dense_part = jnp.einsum("rb,mb->rm", guess_tile, diag_block, precision=highest)
        low_rows = lax.psum_scatter(low_rank, "pan", scatter_dimension=1, tiled=True)
        rhs_rows = lax.dynamic_slice_in_dim(right_side, row_start, own_rows, 1)
        residual = rhs_rows - (dense_part + low_rows)
        residual_full = lax.all_gather(residual, "pan", axis=1, tiled=True)
        residual_tile = lax.dynamic_slice_in_dim(
            residual_full, tile_slot * tile_width, tile_width, 1
        )
        update = jnp.einsum("rb,mb->rm", residual_tile, diag_inverse, precision=highest)
        iterate_rows = iterate_rows + update
    return (iterate_rows, residual)


def solution(mesh):
    placed = (
        P(None, "row"),
        P(None, ("row", "pan")),
        P("row", None, "pan", None),
        P("row", None, "pan", None),
        P(None, "row"),
        P(("row", "pan"), None),
        P(("row", "pan"), None),
    )
    return jax.shard_map(
        on_device,
        mesh=mesh,
        in_specs=placed,
        out_specs=(P(None, ("row", "pan")), P(None, ("row", "pan"))),
        check_vma=False,
    )
```

profile of v0, /device:TPU:1, one launch (start us, length us, event | category | flops | bytes accessed | tf_op | source)
XLA Modules:
  0.0 225.3 jit_solution(9807114171824869542)
XLA Ops:
  7.2 2.1 copy.33
  10.3 15.3 %all-gather.5.cloned.1.call-done = f32[256,1024]{0,1:T(8,128)} async-done(((f32[256,512]{0,1:T(8,128)}), f32[256,1024]{0,1:T(8,128)}) %all-gather.5.cloned.1.call-update) | async-done | bytes 1048592 | tf_op jit(solution)/shard_map/all_gather | solution.py:31
  25.6 12.3 %bitcast_multiply_fusion.1 = f32[128,2,8,256]{0,3,2,1:T(8,128)} fusion(f32[256,2,512,1]{0,2,3,1:T(8,128)} %bitcast.45, f32[2,128,8,512]{3,2,1,0:T(8,128)} %param.9, f32[128,2,8]{0,2,1:T(8,128)S(1)} %and_convert_fusion), kind=kOutput, calls=%fused_computation.5 | convolution fusion | flops 3221749760 | bytes 7348224 | tf_op jit(solution)/shard_map/cikb,rcb->ickr/dot_general | solution.py:33
  37.9 2.2 copy.36
  40.2 39.2 %all_to_all.36 = f32[128,2,8,256]{3,2,1,0:T(8,128)S(1)} all-to-all(f32[128,2,8,256]{3,2,1,0:T(8,128)S(1)} %copy.36), channel_id=1, replica_groups=mesh['row'=64,'pan'=2] {'row'}, dimensions={0} | all-to-all | bytes 4194304 | tf_op jit(solution)/shard_map/all_to_all | solution.py:35
  79.6 2.0 copy-done.5
  81.6 3.8 %convolution_bitcast_fusion.1 = f32[256,2,512]{2,0,1:T(8,128)S(1)} fusion(f32[2,128,8,256]{3,2,1,0:T(8,128)S(1)} %bitcast.46, f32[2,128,8,512]{3,2,1,0:T(8,128)S(1)} %copy-done.5), kind=kOutput, calls=%fused_computation.7 | convolution fusion | flops 3221225472 | bytes 7340032 | tf_op jit(solution)/shard_map/ickm,ickr->rim/dot_general | solution.py:36
  85.8 1.3 copy.39
  87.2 9.2 %reduce-scatter.3.cloned.1.call-done = f32[256,512]{1,0:T(8,128)} async-done(((f32[256,1024]{1,0:T(8,128)}), f32[256,512]{1,0:T(8,128)}) %reduce-scatter.3.cloned.1.call-update) | async-done | bytes 524304 | tf_op jit(solution)/shard_map/reduce_scatter | solution.py:40
  96.4 3.9 %fusion.8 = f32[256,512]{1,0:T(8,128)} fusion(f32[256,512]{1,0:T(8,128)} %reduce-scatter.3.cloned.1.call-done, f32[512,512]{1,0:T(8,128)S(1)} %copy-done, f32[256,1024]{0,1:T(8,128)S(1)} %copy-done.4, s32[]{:T(128)S(6)} %select_n.17, f32[256,1024]{1,0:T(8,128)} %param.7, s32[]{:T(128)S(6)} %select_n.15), kind=kOutput, calls=%fused_computation.12 | convolution fusion | flops 805568512 | bytes 3145736 | tf_op jit(solution)/shard_map/rb,mb->rm/dot_general | solution.py:39
  100.4 13.2 %all-gather.7.cloned.1.call-done = f32[256,1024]{1,0:T(8,128)} async-done(((f32[256,512]{1,0:T(8,128)}), f32[256,1024]{1,0:T(8,128)}) %all-gather.7.cloned.1.call-update) | async-done | bytes 1048592 | tf_op jit(solution)/shard_map/all_gather | solution.py:43
  113.5 3.1 %convolution_add_fusion.2 = f32[256,512]{1,0:T(8,128)} fusion(f32[256,512]{1,0:T(8,128)} %param.8, f32[512,512]{1,0:T(8,128)S(1)} %copy-done.2, f32[256,1024]{1,0:T(8,128)} %all-gather.7.cloned.1.call-done, s32[]{:T(128)S(6)} %select_n.17), kind=kOutput, calls=%fused_computation.10 | convolution fusion | flops 805437440 | bytes 2621444 | tf_op jit(solution)/shard_map/rb,mb->rm/dot_general | solution.py:47
  116.9 13.0 %all-gather.9.cloned.1.call-done = f32[256,1024]{1,0:T(8,128)} async-done(((f32[256,512]{1,0:T(8,128)}), f32[256,1024]{1,0:T(8,128)}) %all-gather.9.cloned.1.call-update) | async-done | bytes 1048592 | tf_op jit(solution)/shard_map/all_gather | solution.py:31
  129.8 2.1 reshape.49
  132.0 9.3 %bitcast_multiply_fusion = f32[128,2,8,256]{0,3,2,1:T(8,128)} fusion(f32[2,128,8,512]{3,2,1,0:T(8,128)} %param.9, f32[256,2,512,1]{2,1,0,3:T(2,128)S(1)} %bitcast.44, f32[128,2,8]{0,2,1:T(8,128)S(1)} %and_convert_fusion), kind=kOutput, calls=%fused_computation.4 | convolution fusion | flops 3221749760 | bytes 7348224 | tf_op jit(solution)/shard_map/cikb,rcb->ickr/dot_general | solution.py:33
  141.2 2.2 copy.42
  143.5 39.2 %all_to_all.37 = f32[128,2,8,256]{3,2,1,0:T(8,128)S(1)} all-to-all(f32[128,2,8,256]{3,2,1,0:T(8,128)S(1)} %copy.42), channel_id=1, replica_groups=mesh['row'=64,'pan'=2] {'row'}, dimensions={0} | all-to-all | bytes 4194304 | tf_op jit(solution)/shard_map/all_to_all | solution.py:35
  182.9 2.0 copy-done.6
  184.9 3.8 %convolution_bitcast_fusion = f32[2,32,8,512]{3,2,1,0:T(8,128)S(1)} fusion(f32[2,128,8,256]{3,2,1,0:T(8,128)S(1)} %bitcast.47, f32[2,128,8,512]{3,2,1,0:T(8,128)S(1)} %copy-done.6), kind=kOutput, calls=%fused_computation.6 | convolution fusion | flops 3221225472 | bytes 7340032 | tf_op jit(solution)/shard_map/ickm,ickr->rim/dot_general | solution.py:36
  188.7 1.1 copy.53
  189.9 9.2 %reduce-scatter.5.cloned.1.call-done = f32[256,512]{1,0:T(8,128)} async-done(((f32[256,1024]{1,0:T(8,128)}), f32[256,512]{1,0:T(8,128)}) %reduce-scatter.5.cloned.1.call-update) | async-done | bytes 524304 | tf_op jit(solution)/shard_map/reduce_scatter | solution.py:40
  199.1 3.2 %fusion.9 = f32[256,512]{1,0:T(8,128)} fusion(f32[256,512]{1,0:T(8,128)} %reduce-scatter.5.cloned.1.call-done, f32[512,512]{1,0:T(8,128)S(1)} %copy-done, f32[256,1024]{1,0:T(8,128)} %all-gather.9.cloned.1.call-done, s32[]{:T(128)S(6)} %select_n.17, f32[256,1024]{1,0:T(8,128)} %param.7, s32[]{:T(128)S(6)} %select_n.15), kind=kOutput, calls=%fused_computation.13 | convolution fusion | flops 805568512 | bytes 3145736 | tf_op jit(solution)/shard_map/rb,mb->rm/dot_general | solution.py:39
  202.4 13.2 %all-gather.11.cloned.1.call-done = f32[256,1024]{1,0:T(8,128)} async-done(((f32[256,512]{1,0:T(8,128)}), f32[256,1024]{1,0:T(8,128)}) %all-gather.11.cloned.1.call-update) | async-done | bytes 1048592 | tf_op jit(solution)/shard_map/all_gather | solution.py:43
  215.6 2.9 %convolution_add_fusion = f32[256,512]{1,0:T(8,128)} fusion(f32[256,512]{1,0:T(8,128)S(1)} %copy-done.1, f32[512,512]{1,0:T(8,128)S(1)} %copy-done.3, f32[256,1024]{1,0:T(8,128)} %all-gather.11.cloned.1.call-done, s32[]{:T(128)S(6)} %select_n.17), kind=kOutput, calls=%fused_computation.8 | convolution fusion | flops 805437440 | bytes 2621444 | tf_op jit(solution)/shard_map/rb,mb->rm/dot_general | solution.py:47
  (31 shorter events, 2.1 us)
Async XLA Ops:
  7.2 89.3 %copy-start = (f32[512,512]{1,0:T(8,128)S(1)}, f32[512,512]{1,0:T(8,128)}, u32[]{:S(2)}) copy-start(f32[512,512]{1,0:T(8,128)} %param.12) | copy-start | bytes 3145732
  7.2 18.4 %all-gather.5.cloned.1.call-start = ((), (), s32[]{:S(2)}) async-start(), calls=%async_computation.4 | async-start | bytes 1572864 | tf_op jit(solution)/shard_map/all_gather | solution.py:31
  9.4 87.0 %reduce-scatter.3.cloned.1.call-start = ((), (), s32[]{:S(2)}) async-start(), calls=%async_computation.5 | async-start | bytes 1572864 | tf_op jit(solution)/shard_map/reduce_scatter | solution.py:40
  79.4 2.2 copy-start.5
  85.8 10.7 %copy-start.4 = (f32[256,1024]{0,1:T(8,128)S(1)}, f32[256,1024]{0,1:T(8,128)}, u32[]{:S(2)}) copy-start(f32[256,1024]{0,1:T(8,128)} %all-gather.5.cloned.1.call-done) | copy-start | bytes 3145732
  87.1 26.4 %copy-start.2 = (f32[512,512]{1,0:T(8,128)S(1)}, f32[512,512]{1,0:T(8,128)}, u32[]{:S(2)}) copy-start(f32[512,512]{1,0:T(8,128)} %param.13) | copy-start | bytes 3145732
  87.1 26.4 %all-gather.7.cloned.1.call-start = ((), (), s32[]{:S(2)}) async-start(), calls=%async_computation.6 | async-start | bytes 1572864 | tf_op jit(solution)/shard_map/all_gather | solution.py:43
  100.3 29.5 %all-gather.9.cloned.1.call-start = ((), (), s32[]{:S(2)}) async-start(), calls=%async_computation.7 | async-start | bytes 1572864 | tf_op jit(solution)/shard_map/all_gather | solution.py:31
  116.6 82.5 %reduce-scatter.5.cloned.1.call-start = ((), (), s32[]{:S(2)}) async-start(), calls=%async_computation.8 | async-start | bytes 1572864 | tf_op jit(solution)/shard_map/reduce_scatter | solution.py:40
  182.7 2.2 copy-start.6
  189.8 25.8 %copy-start.1 = (f32[256,512]{1,0:T(8,128)S(1)}, f32[256,512]{1,0:T(8,128)}, u32[]{:S(2)}) copy-start(f32[256,512]{1,0:T(8,128)} %convolution_add_fusion.2) | copy-start | bytes 1572868
  189.8 25.8 %copy-start.3 = (f32[512,512]{1,0:T(8,128)S(1)}, f32[512,512]{1,0:T(8,128)}, u32[]{:S(2)}) copy-start(f32[512,512]{1,0:T(8,128)} %param.13) | copy-start | bytes 3145732
  189.8 25.7 %all-gather.11.cloned.1.call-start = ((), (), s32[]{:S(2)}) async-start(), calls=%async_computation.9 | async-start | bytes 1572864 | tf_op jit(solution)/shard_map/all_gather | solution.py:43
Sparse Core Ops, SparseCore 0:
  10.2 15.3 all-gather.4
  87.2 9.1 reduce-scatter.2
  100.4 13.0 all-gather.6
  116.7 13.0 all-gather.8
  189.9 9.1 reduce-scatter.4
  202.5 13.0 all-gather.10
where the time goes:
time: 226 us; the launch traced here: 225 us
  blocking collectives  78.4 us (35%)
  waiting for transfers between devices  73.2 us (32%)
  matrix products  42.3 us (19%)
  local copies, waits for them, and re-layouts  15.8 us (7%)
  between operations  14.3 us (6%)
    all_to_all x2, blocking collectives, on_device(): lax.all_to_all(projected, 'row', split_axis=0, concat_axis=1, tiled=True)  78.4 us
    all_gather x2, waiting for transfers between devices, on_device(): guess_full = lax.all_gather(iterate_rows, 'pan', axis=1, tiled=True)  28.3 us
    all_gather x2, waiting for transfers between devices, on_device(): residual_full = lax.all_gather(residual, 'pan', axis=1, tiled=True)  26.4 us
    dot_general x2, matrix products, on_device(): jnp.einsum('cikb,rcb->ickr', v_factor, guess_tiles, precision=highest)  21.6 us
    reduce_scatter x2, waiting for transfers between devices, on_device(): lax.psum_scatter(low_rank, 'pan', scatter_dimension=1, tiled=True)  18.5 us
    dot_general x2, matrix products, on_device(): jnp.einsum('ickm,ickr->rim', u_factor, received, precision=highest)  7.64 us
    dot_general x2, matrix products, on_device(): jnp.einsum('rb,mb->rm', guess_tile, diag_block, precision=highest)  7.07 us
    unnamed x15, local copies, waits for them, and re-layouts  6.15 us
  transfers between devices with their start and end apart: 6, of which 6 were waited for; matrix products, arithmetic and copies ran while one was open for 0% of the time, Pallas kernels for 0%

commit v1 on v0

v1 whole, which is shorter than its diff:
```python
import jax
import jax.numpy as jnp
from jax import lax
from jax.experimental import pallas as pl
from jax.experimental.pallas import tpu as pltpu
from jax.sharding import PartitionSpec as P

ITERS = 2
SIDE = 4
GROUPS = 16
BLOCKS = 8
HALF = 8
RANK = 16
WIDTH = 512
RHS = 256
MESH = pl.DeviceIdType.MESH


def halves(x):
    high = x.astype(jnp.bfloat16)
    low = (x - high.astype(jnp.float32)).astype(jnp.bfloat16)
    return high, low


def dot(a, b):
    return jnp.dot(a, b, preferred_element_type=jnp.float32)


def far_first(t):
    return jnp.where(t == 0, 2, jnp.where(t == 1, 1, jnp.where(t == 2, 3, 0)))


def kernel(
    ranks, v_hbm, u_hbm, rhs_hbm, guess_hbm, diag_hbm, inverse_hbm,
    solution_out, residual_out,
    vbuf, ubuf, ut, pbuf, rbuf, diag, inverse, wide, rhs_t, guess_t, gh, gl, dense, acc,
    load_sem, vsend, vrecv, usend, urecv, send_sem, recv_sem,
):
    row = lax.axis_index("row")
    pan = lax.axis_index("pan")
    other = 1 - pan
    tile = row * 2 + pan
    my_x = lax.rem(row, SIDE)
    my_y = lax.rem(row // SIDE, SIDE)
    my_z = row // (SIDE * SIDE)
    my_group = row // SIDE

    loads = [
        pltpu.make_async_copy(v_hbm.at[pan], vbuf.at[:, pan], load_sem.at[0]),
        pltpu.make_async_copy(guess_hbm, wide.at[0], load_sem.at[1]),
        pltpu.make_async_copy(
            rhs_hbm.at[:, pl.ds(pl.multiple_of(pan * WIDTH, WIDTH), WIDTH)], wide.at[1], load_sem.at[2]
        ),
        pltpu.make_async_copy(diag_hbm, diag, load_sem.at[3]),
        pltpu.make_async_copy(inverse_hbm, inverse, load_sem.at[4]),
        pltpu.make_async_copy(u_hbm.at[pan], ubuf.at[:, pan], load_sem.at[5]),
    ]
    for load in loads:
        load.start()

    barrier = pltpu.get_barrier_semaphore()

    def greet(t, carry):
        target = lax.rem(tile + t, GROUPS * BLOCKS)
        pl.semaphore_signal(
            barrier, inc=1, device_id=(target // 2, lax.rem(target, 2)), device_id_type=MESH
        )
        return carry

    lax.fori_loop(1, GROUPS * BLOCKS, greet, 0)

    loads[1].wait()
    start = wide[0].T
    guess_t[...] = start
    high, low = halves(start)
    gh[...] = high
    gl[...] = low

    pl.semaphore_wait(barrier, GROUPS * BLOCKS - 1)

    def group_at(s, sign):
        dz = far_first(s // SIDE)
        dy = far_first(lax.rem(s, SIDE))
        z = lax.rem(my_z + sign * dz + SIDE, SIDE)
        y = lax.rem(my_y + sign * dy + SIDE, SIDE)
        return z * SIDE + y

    def v_piece(g):
        return pltpu.make_async_remote_copy(
            src_ref=v_hbm.at[other, pl.ds(g * BLOCKS, BLOCKS)],
            dst_ref=vbuf.at[pl.ds(g * BLOCKS, BLOCKS), pan],
            send_sem=vsend,
            recv_sem=vrecv.at[g],
            device_id=(row, other),
            device_id_type=MESH,
        )

    def start_piece(s, carry):
        v_piece(group_at(s, 1)).start()
        return carry

    lax.fori_loop(0, GROUPS, start_piece, 0)
    u_swap = pltpu.make_async_remote_copy(
        src_ref=u_hbm.at[other],
        dst_ref=ubuf.at[:, pan],
        send_sem=usend,
        recv_sem=urecv,
        device_id=(row, other),
        device_id_type=MESH,
    )
    u_swap.start()
    loads[0].wait()

    component = lax.broadcasted_iota(jnp.int32, (RANK, RHS), 0)

    for it in range(ITERS):

        def project(s, carry, it=it):
            g = group_at(s, 1)
            if it == 0:
                piece = vbuf.at[pl.ds(g * BLOCKS, BLOCKS), other]
                pltpu.make_async_copy(piece, piece, vrecv.at[g]).wait()
            first = pl.multiple_of(g * BLOCKS, BLOCKS)
            v = vbuf[pl.ds(first, BLOCKS)].reshape(BLOCKS * RANK, WIDTH)
            vh, vl = halves(v)
            p = dot(vh, gh[...]) + dot(vh, gl[...]) + dot(vl, gh[...])
            for b in range(BLOCKS):
                dest = first + b
                rank = jnp.where(dest == tile, 0, ranks[dest, pan])
                pbuf[it, dest] = jnp.where(component < rank, p[b * RANK:(b + 1) * RANK], 0.0)
            for t in range(SIDE):
                shift = (2, 1, 3, 0)[t]
                x = lax.rem(my_x + shift, SIDE)
                to_row = g * SIDE + x
                for core in range(2):
                    to_pan = lax.rem(pan + 1 + core, 2)
                    dest = to_row * 2 + to_pan

                    def remote(to_row=to_row, to_pan=to_pan, dest=dest):
                        pltpu.make_async_remote_copy(
                            src_ref=pbuf.at[it, dest],
                            dst_ref=rbuf.at[it, tile],
                            send_sem=send_sem.at[it],
                            recv_sem=recv_sem.at[it, my_group],
                            device_id=(to_row, to_pan),
                            device_id_type=MESH,
                        ).start()

                    if shift == 0 and core == 1:
                        pl.when(dest != tile)(remote)

                        @pl.when(dest == tile)
                        def _(dest=dest):
                            pltpu.make_async_copy(
                                pbuf.at[it, dest], rbuf.at[it, tile], recv_sem.at[it, my_group]
                            ).start()
                    else:
                        remote()
            return carry

        lax.fori_loop(0, GROUPS, project, 0)

        if it == 0:
            loads[2].wait()
            rhs_t[...] = wide[1].T
            loads[3].wait()
            loads[4].wait()

        def dense_block(b, carry):
            rows = pl.ds(pl.multiple_of(b * 128, 128), 128)
            dh, dl = halves(diag[rows, :])
            dense[rows, :] = rhs_t[rows, :] - (
                dot(dh, gh[...]) + dot(dh, gl[...]) + dot(dl, gh[...])
            )
            return carry

        lax.fori_loop(0, WIDTH // 128, dense_block, 0)

        if it == 0:
            loads[5].wait()
            u_swap.wait_recv()

            def turn(g, carry):
                block = ubuf[pl.ds(pl.multiple_of(g * BLOCKS, BLOCKS), BLOCKS)].reshape(BLOCKS * RANK, WIDTH)
                uh, ul = halves(block.T)
                ut[g, :, 0:128] = uh
                ut[g, :, 128:256] = ul
                return carry

            lax.fori_loop(0, GROUPS, turn, 0)

        acc[...] = jnp.zeros_like(acc)

        def gather(s, carry, it=it):
            g = group_at(s, -1)
            block = rbuf.at[it, pl.ds(g * BLOCKS, BLOCKS)]
            pltpu.make_async_copy(block, block, recv_sem.at[it, g]).wait()
            r = rbuf[it, pl.ds(pl.multiple_of(g * BLOCKS, BLOCKS), BLOCKS)].reshape(BLOCKS * RANK, RHS)
            rh, rl = halves(r)
            both = ut[g]
            acc[...] += dot(both, jnp.concatenate([rh, rh], axis=0)) + dot(both[:, 0:128], rl)
            return carry

        lax.fori_loop(0, GROUPS, gather, 0)

        residual = dense[...] - acc[...]
        acc[...] = residual
        rh, rl = halves(residual)

        def update_block(b, carry):
            rows = pl.ds(pl.multiple_of(b * 128, 128), 128)
            ih, il = halves(inverse[rows, :])
            fresh = guess_t[rows, :] + (dot(ih, gh[...]) + dot(ih, gl[...]) + dot(il, gh[...]))
            guess_t[rows, :] = fresh
            return carry

        gh[...] = rh
        gl[...] = rl
        lax.fori_loop(0, WIDTH // 128, update_block, 0)
        if it < ITERS - 1:
            high, low = halves(guess_t[...])
            gh[...] = high
            gl[...] = low

    residual_out[...] = acc[...].T
    solution_out[...] = guess_t[...].T

    most = pl.ds(0, GROUPS * BLOCKS - 1)
    for it in range(ITERS):
        pltpu.make_async_copy(pbuf.at[it, most], pbuf.at[it, most], send_sem.at[it]).wait()
    pltpu.make_async_copy(v_hbm.at[other], vbuf.at[:, other], vsend).wait()
    u_swap.wait_send()


def on_device(right_side, initial_guess, v_factor, u_factor, tile_ranks, diag_block, diag_inverse):
    f32 = jnp.float32
    bf16 = jnp.bfloat16
    anywhere = pl.BlockSpec(memory_space=pl.ANY)
    vmem = pl.BlockSpec(memory_space=pltpu.VMEM)
    out = jax.ShapeDtypeStruct((RHS, WIDTH), f32)
    tiles = GROUPS * BLOCKS
    return pl.pallas_call(
        kernel,
        out_shape=(out, out),
        in_specs=[pl.BlockSpec(memory_space=pltpu.SMEM)] + [anywhere] * 6,
        out_specs=(vmem, vmem),
        scratch_shapes=[
            pltpu.VMEM((tiles, 2, HALF, WIDTH), f32),
            pltpu.VMEM((tiles, 2, HALF, WIDTH), f32),
            pltpu.VMEM((GROUPS, WIDTH, 256), bf16),
            pltpu.VMEM((ITERS, tiles, RANK, RHS), f32),
            pltpu.VMEM((ITERS, tiles, RANK, RHS), f32),
            pltpu.VMEM((WIDTH, WIDTH), f32),
            pltpu.VMEM((WIDTH, WIDTH), f32),
            pltpu.VMEM((2, RHS, WIDTH), f32),
            pltpu.VMEM((WIDTH, RHS), f32),
            pltpu.VMEM((WIDTH, RHS), f32),
            pltpu.VMEM((WIDTH, RHS), bf16),
            pltpu.VMEM((WIDTH, RHS), bf16),
            pltpu.VMEM((WIDTH, RHS), f32),
            pltpu.VMEM((WIDTH, RHS), f32),
            pltpu.SemaphoreType.DMA((6,)),
            pltpu.SemaphoreType.DMA,
            pltpu.SemaphoreType.DMA((GROUPS,)),
            pltpu.SemaphoreType.DMA,
            pltpu.SemaphoreType.DMA,
            pltpu.SemaphoreType.DMA((ITERS,)),
            pltpu.SemaphoreType.DMA((ITERS, GROUPS)),
        ],
        compiler_params=pltpu.CompilerParams(
            collective_id=0, has_side_effects=True, vmem_limit_bytes=56 * 1024 * 1024
        ),
    )(tile_ranks, v_factor, u_factor, right_side, initial_guess, diag_block, diag_inverse)


def solution(mesh):
    placed = (
        P(None, "row"),
        P(None, ("row", "pan")),
        P("row", None, "pan", None),
        P("row", None, "pan", None),
        P(None, "row"),
        P(("row", "pan"), None),
        P(("row", "pan"), None),
    )
    return jax.shard_map(
        on_device,
        mesh=mesh,
        in_specs=placed,
        out_specs=(P(None, ("row", "pan")), P(None, ("row", "pan"))),
        check_vma=False,
    )
```

time: 226 us -> 92.9 us (0.41)
  Pallas kernels: 0 us -> 86.4 us
  blocking collectives: 78.4 us -> 0 us
  waiting for transfers between devices: 73.2 us -> 0 us
  matrix products: 42.3 us -> 0 us
  between operations: 14.3 us -> 0.64 us
  local copies, waits for them, and re-layouts: 15.8 us -> 5.15 us
    pallas_call x0 -> x1, Pallas kernels: none -> 86.4 us  [on_device(): pl.pallas_call(kernel, out_shape=(out, out), in_specs=[pl.BlockSpec(memor...]
    all_to_all x2 -> x0, blocking collectives: 78.4 us -> none  [on_device(): lax.all_to_all(projected, 'row', split_axis=0, concat_axis=1, tiled=True)]
    all_gather x4 -> x0, waiting for transfers between devices: 54.7 us -> none  [the longest x2 28.3 us: on_device(): guess_full = lax.all_gather(iterate_rows, 'pan', axis=1, tiled=True)]
    dot_general x8 -> x0, matrix products: 42.3 us -> none  [the longest x2 21.6 us: on_device(): jnp.einsum('cikb,rcb->ickr', v_factor, guess_tiles, precision=highest)]
    reduce_scatter x2 -> x0, waiting for transfers between devices: 18.5 us -> none  [on_device(): lax.psum_scatter(low_rank, 'pan', scatter_dimension=1, tiled=True)]
    reshape x3 -> x0, local copies, waits for them, and re-layouts: 4.5 us -> none  [the longest x2 2.39 us: on_device(): low_rank = low_rank.reshape(rhs_count, tile_rows * tile_width)]
    mul x2 -> x0, local copies, waits for them, and re-layouts: 4.47 us -> none  [on_device(): projected = projected * rank_mask[:, :, :, None]]
    unnamed x15 -> x3, local copies, waits for them, and re-layouts: 6.15 us -> 5.15 us
  transfers between devices with their start and end apart: 6 -> 0, of which waited for: 6 -> 0; matrix products, arithmetic and copies ran while one was open for 0% -> 0% of each run, Pallas kernels for 0% -> 0%
where the time goes in v1:
time: 92.9 us; the launch traced here: 92.2 us
  Pallas kernels  86.4 us (93%)
  local copies, waits for them, and re-layouts  5.15 us (6%)
    pallas_call x1, Pallas kernels, on_device(): pl.pallas_call(kernel, out_shape=(out, out), in_specs=[pl.BlockSpec(memor...  86.4 us
    unnamed x3, local copies, waits for them, and re-layouts  5.15 us

profile of v1, /device:TPU:1, one launch (start us, length us, event | category | flops | bytes accessed | tf_op | source)
XLA Modules:
  0.0 92.2 jit_solution(2598618863232916790)
XLA Ops:
  0.6 1.4 %copy.9.ranks = s32[128,2]{1,0:T(8,128)} copy(s32[128,2]{0,1:T(2,128)} %param.11) | data formatting | bytes 2048 | tf_op args[4]
  2.0 86.4 %shard_map.86 = (f32[256,512]{1,0:T(8,128)}, f32[256,512]{1,0:T(8,128)}) custom-call(s32[128,2]{1,0:T(8,128)} %copy.9.ranks, f32[2,128,8,512]{3,2,1,0:T(8,128)} %v_hbm.1, f32[2,128,8,512]{3,2,1,0:T(8,128)} %u_hbm.1, f32[256,1024]{1,0:T(8,128)} %rhs_hbm.1, f32[256,512]{1,0:T(8,128)} %guess_hbm.1, f32[512,512]{1,0:T(8,128)} %diag_hbm.1, f32[512,512]{1,0:T(8,128)} %inverse_hbm.1), custom_call_target="tpu_custom_call" | custom-call | tf_op jit(solution)/shard_map/pallas_call | solution.py:242
  88.5 1.9 %copy.12 = f32[256,512]{1,0:T(8,128)} copy(f32[256,512]{1,0:T(8,128)} %get-tuple-element.4) | data formatting | bytes 1048576
  90.3 1.9 %copy.13 = f32[256,512]{1,0:T(8,128)} copy(f32[256,512]{1,0:T(8,128)} %get-tuple-element.5) | data formatting | bytes 1048576
